TPU v7x, 256 devices: a whole 4x4x8 slice. The times are simulated.
256 devices in a mesh: state: 8 (over z), tile: 32 (over x, y, core).
Axes of the slice: x: 4, y: 4, z: 8, core: 2. Of those that a mesh axis runs over, the one named last changes fastest.
Arguments:
- bands: bfloat16 [8, 240, 524288], P('state', None, 'tile')
- block_slot: int32 [8, 4096], P('state', 'tile'), may hold values from 0 to 7
- tile_counties: int32 [8, 256], P('state', 'tile'), may hold values from 0 to 383, as said below
- county_place: int32 [8, 384], P('state'), may hold values from 0 to 383, as said below
- label: int32 [8, 384], P('state', 'tile'), may hold values from -200 to 200
- w_first: bfloat16 [64, 240], replicated, may hold values from -0.375 to 0.375
- taps: float32 [3, 64], replicated, may hold values from -2 to 2
- w_second: bfloat16 [128, 64], replicated, may hold values from -0.75 to 0.75
- w_third: bfloat16 [128, 128], replicated, may hold values from -0.5 to 0.5
- w_head: bfloat16 [128], replicated, may hold values from -0.5 to 0.5
Outputs:
- county_mean: float32 [8, 384], P('state', 'tile')
- weight_grads: float32 [40256], replicated
Inputs may be any that keep to these rules, and one draw needn't show every extreme that they name: `county_place`: each row is an ordering of the counties of one state region; the county at place p is owned by tile index p // 12 of that region. `tile_counties`: tile t's list names counties of its own state region owned by tile indices t, t + 1, ..., t + 4 - 1 (mod the tile axis's size); at most 4 entries of a list are owned by one tile index, and exactly 4 by t itself.
All inputs are finite; a program needn't handle non-finite values.
Results may differ from a plain program's by a relative error of at most 0.00064.
Values sent between devices are 32-bit elements; how exact they have to be, the bound alone decides.
No kernel may reach another device: no remote copies, remote signals or barrier semaphores. Data moves between devices by JAX's collectives and lax.ppermute only.
A program may use at most 128 MiB of HBM per device.

v0:
```python
import jax
import jax.numpy as jnp
from jax import lax
from jax.sharding import PartitionSpec as P

MOST = 4
REACH = 4


def from_behind(value, axis, by):
    peers = lax.axis_size(axis)
    return lax.ppermute(value, axis, [(i, (i + by) % peers) for i in range(peers)])


def silu_parts(value):
    sig = jax.nn.sigmoid(value)
    return (value * sig, sig * (1.0 + value * (1.0 - sig)))


def along_rows(field, weights, row_len):
    chans, count = field.shape
    grid = field.reshape(chans, count // row_len, row_len)
    padded = jnp.pad(grid, ((0, 0), (0, 0), (1, 1)))
    out = (
        weights[0][:, None, None] * padded[:, :, :-2]
        + weights[1][:, None, None] * grid
        + weights[2][:, None, None] * padded[:, :, 2:]
    )
    return out.reshape(chans, count)


def tap_grads(field, upstream, row_len):
    chans, count = field.shape
    grid = field.reshape(chans, count // row_len, row_len)
    padded = jnp.pad(grid, ((0, 0), (0, 0), (1, 1)))
    above = upstream.reshape(grid.shape)
    return jnp.stack(
        [
            jnp.sum(above * padded[:, :, :-2], axis=(1, 2)),
            jnp.sum(above * grid, axis=(1, 2)),
            jnp.sum(above * padded[:, :, 2:], axis=(1, 2)),
        ]
    )


def contract_last(left, right):
    return lax.dot_general(
        left, right, (((1,), (1,)), ((), ())), preferred_element_type=jnp.float32
    )


def contract_first(left, right):
    return lax.dot_general(
        left, right, (((0,), (0,)), ((), ())), preferred_element_type=jnp.float32
    )


def forward(pixels, w_first, taps, w_second, w_third, w_head, row_len):
    h_one = jnp.dot(w_first, pixels, preferred_element_type=jnp.float32)
    s_one = along_rows(h_one, taps, row_len)
    a_one = silu_parts(s_one)[0].astype(jnp.bfloat16)
    h_two = jnp.dot(w_second, a_one, preferred_element_type=jnp.float32)
    a_two = silu_parts(h_two)[0].astype(jnp.bfloat16)
    h_three = jnp.dot(w_third, a_two, preferred_element_type=jnp.float32)
    a_three = (silu_parts(h_three)[0] + a_two.astype(jnp.float32)).astype(jnp.bfloat16)
    yhat = jnp.dot(w_head, a_three, preferred_element_type=jnp.float32)
    return (h_one, s_one, a_one, h_two, a_two, h_three, a_three, yhat)


def backward(pixels, saved, taps, w_second, w_third, w_head, cotangent, row_len):
    h_one, s_one, a_one, h_two, a_two, h_three, a_three, yhat = saved
    grad_in = cotangent.astype(jnp.bfloat16)
    d_head = jnp.dot(a_three, grad_in, preferred_element_type=jnp.float32)
    d_a3 = w_head.astype(jnp.float32)[:, None] * grad_in.astype(jnp.float32)[None, :]
    d_h3 = (d_a3 * silu_parts(h_three)[1]).astype(jnp.bfloat16)
    d_third = contract_last(d_h3, a_two)
    d_a2 = contract_first(w_third, d_h3) + d_a3
    d_h2 = (d_a2 * silu_parts(h_two)[1]).astype(jnp.bfloat16)
    d_second = contract_last(d_h2, a_one)
    d_a1 = contract_first(w_second, d_h2)
    d_s1 = d_a1 * silu_parts(s_one)[1]
    d_taps = tap_grads(h_one, d_s1, row_len)
    d_h1 = along_rows(d_s1, jnp.stack([taps[2], taps[1], taps[0]]), row_len).astype(jnp.bfloat16)
    d_first = contract_last(d_h1, pixels)
    return jnp.concatenate(
        [d_first.reshape(-1), d_taps.reshape(-1), d_second.reshape(-1), d_third.reshape(-1), d_head]
    )


def slot_stats(yhat, slots, slot_count):
    blocks = slots.shape[0]
    row_len = yhat.shape[0] // blocks
    member = (slots[None, :] == jnp.arange(slot_count, dtype=jnp.int32)[:, None]).astype(
        jnp.float32
    )
    block_sums = jnp.sum(yhat.reshape(blocks, row_len), axis=1)
    return (
        jnp.sum(member * block_sums[None, :], axis=1),
        jnp.sum(member, axis=1) * row_len,
        member,
    )


def place_of(counties, table):
    hits = counties[:, None] == jnp.arange(table.shape[0], dtype=jnp.int32)[None, :]
    return jnp.sum(jnp.where(hits, table[None, :], 0), axis=1)


def judge(sums, counts, labels, devices):
    denom = jnp.maximum(counts, 1.0)
    mean = sums / denom
    live = (counts > 0.5).astype(jnp.float32)
    target = labels.astype(jnp.float32) * 0.01
    return (mean, live * 2.0 * (mean - target) / (devices * denom))


def pixel_cotangent(member, slot_adjoint, row_len):
    block_adjoint = jnp.sum(member * slot_adjoint[:, None], axis=0)
    return jnp.broadcast_to(block_adjoint[:, None], (block_adjoint.shape[0], row_len)).reshape(-1)


def settle(sums, counts, codes, labels, devices):
    flat_codes = codes.reshape(-1)
    owned = jnp.arange(1, labels.shape[0] + 1, dtype=jnp.int32).astype(jnp.float32)
    hit = (flat_codes[:, None] == owned[None, :]).astype(jnp.float32)
    total = jnp.sum(hit * sums.reshape(-1)[:, None], axis=0)
    number = jnp.sum(hit * counts.reshape(-1)[:, None], axis=0)
    mean, adjoint = judge(total, number, labels, devices)
    back = jnp.sum(hit * adjoint[None, :], axis=1).reshape(codes.shape)
    return (mean, back)


def packed(select, values, rows):
    return jnp.sum(select * values[:, None], axis=0).reshape(rows, -1)


def on_device(
    bands, block_slot, tile_counties, county_place, label, w_first, taps, w_second, w_third, w_head
):
    pixels = bands[0]
    slots = block_slot[0]
    row_len = pixels.shape[1] // slots.shape[0]
    slot_total = tile_counties.shape[1]
    saved = forward(pixels, w_first, taps, w_second, w_third, w_head, row_len)
    slot_sums, slot_counts, member = slot_stats(saved[-1], slots, slot_total)
    table = county_place[0]
    place = place_of(tile_counties[0], table)
    labels_mine = label[0]
    cty_dev = labels_mine.shape[0]
    n_tile = lax.axis_size("tile")
    devices = float(lax.axis_size("state") * n_tile)
    owner = place // cty_dev
    local_code = (place % cty_dev + 1).astype(jnp.float32)
    order = jnp.arange(slot_total, dtype=jnp.int32)
    rank = jnp.sum(
        ((owner[:, None] == owner[None, :]) & (order[None, :] < order[:, None])).astype(jnp.int32),
        axis=1,
    )
    me = lax.axis_index("tile")
    position = (owner - me) % n_tile * MOST + rank
    select = (position[:, None] == jnp.arange(REACH * MOST, dtype=jnp.int32)[None, :]).astype(
        jnp.float32
    )
    out_sums = packed(select, slot_sums, REACH)
    out_counts = packed(select, slot_counts, REACH)
    out_codes = packed(select, local_code, REACH)
    got_sums, got_counts, got_codes = ([], [], [])
    for step in range(REACH):
        if step == 0:
            piece = (out_sums[0], out_counts[0], out_codes[0])
        else:
            piece = from_behind((out_sums[step], out_counts[step], out_codes[step]), "tile", step)
        got_sums.append(piece[0])
        got_counts.append(piece[1])
        got_codes.append(piece[2])
    county_mean, back = settle(
        jnp.stack(got_sums), jnp.stack(got_counts), jnp.stack(got_codes), labels_mine, devices
    )
    rows = []
    for step in range(REACH):
        if step == 0:
            rows.append(back[0])
        else:
            rows.append(from_behind(back[step], "tile", -step))
    returned = jnp.stack(rows).reshape(-1)
    slot_adjoint = jnp.sum(select * returned[None, :], axis=1)
    cotangent = pixel_cotangent(member, slot_adjoint, row_len)
    local_grads = backward(pixels, saved, taps, w_second, w_third, w_head, cotangent, row_len)
    weight_grads = lax.psum(local_grads, ("state", "tile"))
    return (county_mean[None, :], weight_grads)


def solution(mesh):
    in_specs = (
        P("state", None, "tile"),
        P("state", "tile"),
        P("state", "tile"),
        P("state", None),
        P("state", "tile"),
        P(),
        P(),
        P(),
        P(),
        P(),
    )
    out_specs = (P("state", "tile"), P())
    return jax.shard_map(
        on_device, mesh=mesh, in_specs=in_specs, out_specs=out_specs, check_vma=False
    )
```

profile of v0, /device:TPU:1, one launch (start us, length us, event | category | flops | bytes accessed | tf_op | source)
XLA Modules:
  0.0 352.5 jit_solution(9751502985637400692)
XLA Ops:
  8.0 4.7 %fusion.5 = f32[64,128,128]{2,0,1:T(8,128)S(1)} fusion(bf16[64,240]{1,0:T(8,128)(2,1)} %param.15, bf16[1,240,16384]{2,1,0:T(8,128)(2,1)} %param.10), kind=kOutput, calls=%fused_computation.18 | convolution fusion | flops 503316480 | bytes 12089344 | tf_op jit(solution)/shard_map/dot_general | solution.py:59
  12.8 2.4 fusion.18
  15.2 4.6 %multiply_convert_fusion = (bf16[128,16384]{0,1:T(8,128)(2,1)S(1)}, f32[128,16384]{0,1:T(8,128)}) fusion(bf16[64,16384]{1,0:T(8,128)(2,1)S(1)} %fusion.18, bf16[128,64]{0,1:T(8,128)(2,1)S(1)} %copy-done.12), kind=kOutput, calls=%fused_computation.16 | convolution fusion | flops 278921216 | bytes 14696448 | tf_op jit(solution)/shard_map/dot_general | solution.py:62
  19.8 4.6 %add_convert_fusion = (bf16[128,16384]{0,1:T(8,128)(2,1)S(1)}, f32[128,16384]{0,1:T(8,128)}) fusion(bf16[128,16384]{0,1:T(8,128)(2,1)S(1)} %get-tuple-element.37, bf16[128,128]{1,0:T(8,128)(2,1)S(1)} %copy-done), kind=kOutput, calls=%fused_computation.14 | convolution fusion | flops 551550976 | bytes 16809984 | tf_op jit(solution)/shard_map/dot_general | solution.py:64
  24.5 1.9 copy-done.3
  28.5 2.7 collective-permute-start.3
  31.2 1.3 collective-permute-start.4
  32.5 1.7 collective-permute-start.5
  36.1 2.1 collective-permute-start.2
  39.7 2.2 collective-permute-start.8
  42.6 2.0 collective-permute-done.7
  44.6 1.5 collective-permute-done.8
  47.9 2.0 collective-permute-start.10
  50.6 3.8 %collective-permute-done.11 = f32[4]{0:T(128)S(1)} collective-permute-done((f32[4]{0:T(128)S(1)}, f32[4]{0:T(128)S(1)}, u32[]{:S(2)}, u32[]{:S(2)}) %collective-permute-start.11) | collective-permute-done | bytes 48 | tf_op jit(solution)/shard_map/ppermute | solution.py:12
  54.9 10.0 %fusion.4 = bf16[128,16384]{0,1:T(8,128)(2,1)S(1)} fusion(f32[128,16384]{0,1:T(8,128)} %get-tuple-element.40, f32[16384]{0:T(1024)S(1)} %get-tuple-element.18, f32[128]{0:T(128)S(1)} %convert_element_type.84), kind=kLoop, calls=%fused_computation.13 | loop fusion | flops 20971520 | bytes 12648960 | tf_op jit(solution)/shard_map/convert_element_type | solution.py:75
  64.9 1.4 convolution_bitcast_fusion.4
  67.1 7.6 %fusion.2 = bf16[128,16384]{0,1:T(8,128)(2,1)S(1)} fusion(bf16[128,16384]{0,1:T(8,128)(2,1)S(1)} %fusion.4, bf16[128,128]{1,0:T(8,128)(2,1)S(1)} %copy-done, f32[128,16384]{0,1:T(8,128)S(1)} %bitcast.178, f32[16384]{0:T(1024)S(1)} %get-tuple-element.18, f32[128]{0:T(128)S(1)} %convert_element_type.84), kind=kOutput, calls=%fused_computation.5 | convolution fusion | flops 559939584 | bytes 16876032 | tf_op jit(solution)/shard_map/dot_general | solution.py:53
  74.7 3.5 fusion.21
  78.1 2.5 multiply_reduce_fusion.2
  80.6 2.5 copy.55
  83.1 1.3 fusion.41
  86.1 9.2 %fusion.8 = f32[64,240]{1,0:T(8,128)S(1)} fusion(bf16[1,240,16384]{2,1,0:T(8,128)(2,1)} %param.10, f32[64,128,128]{2,0,1:T(8,128)} %bitcast.157, f32[64]{0:T(128)S(1)} %get-tuple-element.14, f32[64]{0:T(128)S(1)} %get-tuple-element.16, f32[64]{0:T(128)S(1)} %get-tuple-element.15), kind=kOutput, calls=%fused_computation.21 | convolution fusion | flops 509607936 | bytes 12120832 | tf_op jit(solution)/shard_map/dot_general | solution.py:47
  96.3 247.7 %all-reduce.4.cloned.1.call-done = f32[40256]{0:T(1024)} async-done(((f32[40256]{0:T(1024)}), f32[40256]{0:T(1024)}) %all-reduce.4.cloned.1.call-update) | async-done | bytes 161040 | tf_op jit(solution)/shard_map/psum | solution.py:189
  344.0 1.6 copy.57
  (85 shorter events, 13.3 us)
Async XLA Ops:
  7.2 12.7 %copy-start = (bf16[128,128]{1,0:T(8,128)(2,1)S(1)}, bf16[128,128]{1,0:T(8,128)(2,1)}, u32[]{:S(2)}) copy-start(bf16[128,128]{1,0:T(8,128)(2,1)} %param.18) | copy-start | bytes 98308
  7.2 336.8 %all-reduce.4.cloned.1.call-start = ((), (), s32[]{:S(2)}) async-start(), calls=%async_computation | async-start | bytes 327680 | tf_op jit(solution)/shard_map/psum | solution.py:189
  12.8 7.1 %copy-start.1 = (f32[64,128,128]{2,0,1:T(8,128)}, f32[64,128,128]{2,0,1:T(8,128)S(1)}, u32[]{:S(2)}) copy-start(f32[64,128,128]{2,0,1:T(8,128)S(1)} %fusion.5) | copy-start | bytes 12582916
  19.8 4.6 %copy-start.5 = (bf16[128,16384]{0,1:T(8,128)(2,1)}, bf16[128,16384]{0,1:T(8,128)(2,1)S(1)}, u32[]{:S(2)}) copy-start(bf16[128,16384]{0,1:T(8,128)(2,1)S(1)} %get-tuple-element.37) | copy-start | bytes 12582916
  19.8 6.6 %copy-start.8 = (bf16[128]{0:T(256)(128)(2,1)S(1)}, bf16[128]{0:T(256)(128)(2,1)}, u32[]{:S(2)}) copy-start(bf16[128]{0:T(256)(128)(2,1)} %param.19) | copy-start | bytes 772
  24.5 3.3 copy-start.11
  24.5 3.4 copy-start.7
  24.5 3.5 copy-start.10
  24.5 21.7 %copy-start.9 = (s32[1,12]{1,0:T(1,128)S(1)}, s32[1,12]{1,0:T(1,128)}, u32[]{:S(2)}) copy-start(s32[1,12]{1,0:T(1,128)} %param.14) | copy-start | bytes 148
  28.5 7.6 %collective-permute-start.3 = (f32[4]{0:T(128)S(1)}, f32[4]{0:T(128)S(1)}, u32[]{:S(2)}, u32[]{:S(2)}) collective-permute-start(f32[4]{0:T(128)S(1)} %get-tuple-element.26), channel_id=1, source_target_pairs={{0,1},{1,2},{2,3},{3,4},{4,5},{5,6},{6,7},{7,8},{8,9},{9,10},{10,1... | collective-permute-start | bytes 56 | tf_op jit(solution)/shard_map/ppermute | solution.py:12
  31.2 7.0 %collective-permute-start.4 = (f32[4]{0:T(128)S(1)}, f32[4]{0:T(128)S(1)}, u32[]{:S(2)}, u32[]{:S(2)}) collective-permute-start(f32[4]{0:T(128)S(1)} %get-tuple-element.25), channel_id=1, source_target_pairs={{0,2},{1,3},{2,4},{3,5},{4,6},{5,7},{6,8},{7,9},{8,10},{9,11},{10,... | collective-permute-start | bytes 56 | tf_op jit(solution)/shard_map/ppermute | solution.py:12
  32.5 6.3 %collective-permute-start.5 = (f32[4]{0:T(128)S(1)}, f32[4]{0:T(128)S(1)}, u32[]{:S(2)}, u32[]{:S(2)}) collective-permute-start(f32[4]{0:T(128)S(1)} %get-tuple-element.24), channel_id=1, source_target_pairs={{0,3},{1,4},{2,5},{3,6},{4,7},{5,8},{6,9},{7,10},{8,11},{9,12},{10... | collective-permute-start | bytes 56 | tf_op jit(solution)/shard_map/ppermute | solution.py:12
  34.3 5.4 %collective-permute-start = (f32[4]{0:T(128)S(1)}, f32[4]{0:T(128)S(1)}, u32[]{:S(2)}, u32[]{:S(2)}) collective-permute-start(f32[4]{0:T(128)S(1)} %get-tuple-element.30), channel_id=1, source_target_pairs={{0,1},{1,2},{2,3},{3,4},{4,5},{5,6},{6,7},{7,8},{8,9},{9,10},{10,1... | collective-permute-start | bytes 56 | tf_op jit(solution)/shard_map/ppermute | solution.py:12
  34.7 7.1 %collective-permute-start.1 = (f32[4]{0:T(128)S(1)}, f32[4]{0:T(128)S(1)}, u32[]{:S(2)}, u32[]{:S(2)}) collective-permute-start(f32[4]{0:T(128)S(1)} %get-tuple-element.29), channel_id=1, source_target_pairs={{0,2},{1,3},{2,4},{3,5},{4,6},{5,7},{6,8},{7,9},{8,10},{9,11},{10,... | collective-permute-start | bytes 56 | tf_op jit(solution)/shard_map/ppermute | solution.py:12
  36.1 6.3 %collective-permute-start.2 = (f32[4]{0:T(128)S(1)}, f32[4]{0:T(128)S(1)}, u32[]{:S(2)}, u32[]{:S(2)}) collective-permute-start(f32[4]{0:T(128)S(1)} %get-tuple-element.28), channel_id=1, source_target_pairs={{0,3},{1,4},{2,5},{3,6},{4,7},{5,8},{6,9},{7,10},{8,11},{9,12},{10... | collective-permute-start | bytes 56 | tf_op jit(solution)/shard_map/ppermute | solution.py:12
  38.3 4.3 %collective-permute-start.6 = (f32[4]{0:T(128)S(1)}, f32[4]{0:T(128)S(1)}, u32[]{:S(2)}, u32[]{:S(2)}) collective-permute-start(f32[4]{0:T(128)S(1)} %get-tuple-element.34), channel_id=1, source_target_pairs={{0,1},{1,2},{2,3},{3,4},{4,5},{5,6},{6,7},{7,8},{8,9},{9,10},{10,1... | collective-permute-start | bytes 56 | tf_op jit(solution)/shard_map/ppermute | solution.py:12
  38.8 5.7 %collective-permute-start.7 = (f32[4]{0:T(128)S(1)}, f32[4]{0:T(128)S(1)}, u32[]{:S(2)}, u32[]{:S(2)}) collective-permute-start(f32[4]{0:T(128)S(1)} %get-tuple-element.33), channel_id=1, source_target_pairs={{0,2},{1,3},{2,4},{3,5},{4,6},{5,7},{6,8},{7,9},{8,10},{9,11},{10,... | collective-permute-start | bytes 56 | tf_op jit(solution)/shard_map/ppermute | solution.py:12
  39.7 6.3 %collective-permute-start.8 = (f32[4]{0:T(128)S(1)}, f32[4]{0:T(128)S(1)}, u32[]{:S(2)}, u32[]{:S(2)}) collective-permute-start(f32[4]{0:T(128)S(1)} %get-tuple-element.32), channel_id=1, source_target_pairs={{0,3},{1,4},{2,5},{3,6},{4,7},{5,8},{6,9},{7,10},{8,11},{9,12},{10... | collective-permute-start | bytes 56 | tf_op jit(solution)/shard_map/ppermute | solution.py:12
  47.0 3.2 collective-permute-start.9
  47.9 2.7 collective-permute-start.10
  49.9 4.5 %collective-permute-start.11 = (f32[4]{0:T(128)S(1)}, f32[4]{0:T(128)S(1)}, u32[]{:S(2)}, u32[]{:S(2)}) collective-permute-start(f32[4]{0:T(128)S(1)} %get-tuple-element.20), channel_id=1, source_target_pairs={{0,29},{1,30},{2,31},{3,0},{4,1},{5,2},{6,3},{7,4},{8,5},{9,6},{10... | collective-permute-start | bytes 56 | tf_op jit(solution)/shard_map/ppermute | solution.py:12
  54.9 10.0 %copy-start.6 = (bf16[128,16384]{0,1:T(8,128)(2,1)S(1)}, bf16[128,16384]{0,1:T(8,128)(2,1)}, u32[]{:S(2)}) copy-start(bf16[128,16384]{0,1:T(8,128)(2,1)} %copy-done.5) | copy-start | bytes 12582916
  54.9 11.4 %slice-start = ((s8[8388608]{0:T(1024)(128)(4,1)}), s8[4194304]{0:T(1024)(128)(4,1)S(1)}, s32[]{:S(2)}) async-start(s8[8388608]{0:T(1024)(128)(4,1)} %bitcast.177), calls=%async_computation.1 | async-start | bytes 8388608
  67.1 7.6 %copy-start.2 = (f32[64,128,128]{2,0,1:T(8,128)S(1)}, f32[64,128,128]{2,0,1:T(8,128)}, u32[]{:S(2)}) copy-start(f32[64,128,128]{2,0,1:T(8,128)} %copy-done.1) | copy-start | bytes 12582916
  (4 other events, 8.8 us)
Sparse Core Ops, SparseCore 0:
  96.5 247.5 all-reduce.3
where the time goes:
time: 353 us; the launch traced here: 352 us
  waiting for transfers between devices  256 us (73%)
  matrix products  38.8 us (11%)
  other arithmetic  16.9 us (5%)
  starting transfers between devices  16.2 us (5%)
  between operations  14.3 us (4%)
  local copies, waits for them, and re-layouts  10.2 us (3%)
    psum x1, waiting for transfers between devices, on_device(): weight_grads = lax.psum(local_grads, ('state', 'tile'))  248 us
    ppermute x12, starting transfers between devices, from_behind(): lax.ppermute(value, axis, [(i, (i + by) % peers) for i in range(peers)])  16.2 us
    dot_general x3, matrix products, contract_last(): lax.dot_general(left, right, (((1,), (1,)), ((), ())), preferred_element_...  12 us
    dot_general x2, matrix products, contract_first(): lax.dot_general(left, right, (((0,), (0,)), ((), ())), preferred_element_...  11 us
    convert_element_type x1, other arithmetic, backward(): d_h3 = (d_a3 * silu_parts(h_three)[1]).astype(jnp.bfloat16)  9.98 us
    ppermute x12, waiting for transfers between devices, from_behind(): lax.ppermute(value, axis, [(i, (i + by) % peers) for i in range(peers)])  8.37 us
  transfers between devices with their start and end apart: 13, of which 7 were waited for; matrix products, arithmetic and copies ran while one was open for 0% of the time, Pallas kernels for 0%

commit v1 on v0

--- a/solution.py
+++ b/solution.py
@@ -186,7 +186,7 @@
     slot_adjoint = jnp.sum(select * returned[None, :], axis=1)
     cotangent = pixel_cotangent(member, slot_adjoint, row_len)
     local_grads = backward(pixels, saved, taps, w_second, w_third, w_head, cotangent, row_len)
-    weight_grads = lax.psum(local_grads, ("state", "tile"))
+    weight_grads = lax.psum(lax.psum(local_grads, "tile"), "state")
     return (county_mean[None, :], weight_grads)
 
 

time: 353 us -> 288 us (0.82); the launches traced: 352 us -> 283 us
  waiting for transfers between devices: 256 us -> 187 us
    psum x1 -> x2, waiting for transfers between devices: 248 us -> 179 us  [on_device(): weight_grads = lax.psum(lax.psum(local_grads, 'tile'), 'state')]
  transfers between devices with their start and end apart: 13 -> 14, of which waited for: 7 -> 8; matrix products, arithmetic and copies ran while one was open for 0% -> 0% of each run, Pallas kernels for 0% -> 0%
where the time goes in v1:
time: 288 us; the launch traced here: 283 us
  waiting for transfers between devices  187 us (65%)
  matrix products  38.8 us (13%)
  other arithmetic  16.9 us (6%)
  starting transfers between devices  16.3 us (6%)
  between operations  14.3 us (5%)
  local copies, waits for them, and re-layouts  10.2 us (4%)
    psum x2, waiting for transfers between devices, on_device(): weight_grads = lax.psum(lax.psum(local_grads, 'tile'), 'state')  179 us
    ppermute x12, starting transfers between devices, from_behind(): lax.ppermute(value, axis, [(i, (i + by) % peers) for i in range(peers)])  16.2 us
    dot_general x3, matrix products, contract_last(): lax.dot_general(left, right, (((1,), (1,)), ((), ())), preferred_element_...  12 us
    dot_general x2, matrix products, contract_first(): lax.dot_general(left, right, (((0,), (0,)), ((), ())), preferred_element_...  11 us
    convert_element_type x1, other arithmetic, backward(): d_h3 = (d_a3 * silu_parts(h_three)[1]).astype(jnp.bfloat16)  9.98 us
    ppermute x12, waiting for transfers between devices, from_behind(): lax.ppermute(value, axis, [(i, (i + by) % peers) for i in range(peers)])  8.37 us
  transfers between devices with their start and end apart: 14, of which 8 were waited for; matrix products, arithmetic and copies ran while one was open for 0% of the time, Pallas kernels for 0%

profile of v1, /device:TPU:1, one launch (start us, length us, event | category | flops | bytes accessed | tf_op | source)
XLA Modules:
  0.0 283.4 jit_solution(11866161644787240334)
XLA Ops:
  8.0 4.7 %fusion.5 = f32[64,128,128]{2,0,1:T(8,128)S(1)} fusion(bf16[64,240]{1,0:T(8,128)(2,1)} %param.15, bf16[1,240,16384]{2,1,0:T(8,128)(2,1)} %param.10), kind=kOutput, calls=%fused_computation.18 | convolution fusion | flops 503316480 | bytes 12089344 | tf_op jit(solution)/shard_map/dot_general | solution.py:59
  12.8 2.4 fusion.18
  15.2 4.6 %multiply_convert_fusion = (bf16[128,16384]{0,1:T(8,128)(2,1)S(1)}, f32[128,16384]{0,1:T(8,128)}) fusion(bf16[64,16384]{1,0:T(8,128)(2,1)S(1)} %fusion.18, bf16[128,64]{0,1:T(8,128)(2,1)S(1)} %copy-done.12), kind=kOutput, calls=%fused_computation.16 | convolution fusion | flops 278921216 | bytes 14696448 | tf_op jit(solution)/shard_map/dot_general | solution.py:62
  19.8 4.6 %add_convert_fusion = (bf16[128,16384]{0,1:T(8,128)(2,1)S(1)}, f32[128,16384]{0,1:T(8,128)}) fusion(bf16[128,16384]{0,1:T(8,128)(2,1)S(1)} %get-tuple-element.37, bf16[128,128]{1,0:T(8,128)(2,1)S(1)} %copy-done), kind=kOutput, calls=%fused_computation.14 | convolution fusion | flops 551550976 | bytes 16809984 | tf_op jit(solution)/shard_map/dot_general | solution.py:64
  24.5 1.9 copy-done.3
  28.5 2.7 collective-permute-start.3
  32.5 1.7 collective-permute-start.5
  36.1 2.1 collective-permute-start.2
  39.7 2.2 collective-permute-start.8
  42.6 2.0 collective-permute-done.7
  44.6 1.5 collective-permute-done.8
  47.9 2.0 collective-permute-start.10
  50.6 3.8 %collective-permute-done.11 = f32[4]{0:T(128)S(1)} collective-permute-done((f32[4]{0:T(128)S(1)}, f32[4]{0:T(128)S(1)}, u32[]{:S(2)}, u32[]{:S(2)}) %collective-permute-start.11) | collective-permute-done | bytes 48 | tf_op jit(solution)/shard_map/ppermute | solution.py:12
  54.9 10.0 %fusion.4 = bf16[128,16384]{0,1:T(8,128)(2,1)S(1)} fusion(f32[128,16384]{0,1:T(8,128)} %get-tuple-element.40, f32[16384]{0:T(1024)S(1)} %get-tuple-element.18, f32[128]{0:T(128)S(1)} %convert_element_type.84), kind=kLoop, calls=%fused_computation.13 | loop fusion | flops 20971520 | bytes 12648960 | tf_op jit(solution)/shard_map/convert_element_type | solution.py:75
  64.9 1.4 convolution_bitcast_fusion.4
  67.1 7.6 %fusion.2 = bf16[128,16384]{0,1:T(8,128)(2,1)S(1)} fusion(bf16[128,16384]{0,1:T(8,128)(2,1)S(1)} %fusion.4, bf16[128,128]{1,0:T(8,128)(2,1)S(1)} %copy-done, f32[128,16384]{0,1:T(8,128)S(1)} %bitcast.178, f32[16384]{0:T(1024)S(1)} %get-tuple-element.18, f32[128]{0:T(128)S(1)} %convert_element_type.84), kind=kOutput, calls=%fused_computation.5 | convolution fusion | flops 559939584 | bytes 16876032 | tf_op jit(solution)/shard_map/dot_general | solution.py:53
  74.7 3.5 %fusion.21 = f32[8,128,8,128]{3,2,1,0:T(8,128)S(1)} fusion(bf16[128,16384]{0,1:T(8,128)(2,1)S(1)} %fusion.2, bf16[128,64]{0,1:T(8,128)(2,1)S(1)} %copy-done.12, f32[64,128,128]{2,0,1:T(8,128)S(1)} %copy-done.2, f32[64]{0:T(128)S(1)} %get-tuple-element.15, f32[64]{0:T(128)S(1)} %get-tuple-element.16, f32[64]{0:T(128)S(1)} %get-tuple-element.14), kind=kOutput, calls=%fused_computation.43 | convolution fusion | flops 282066944 | bytes 12600064 | tf_op jit(solution)/shard_map/dot_general | solution.py:53
  78.1 2.5 multiply_reduce_fusion.2
  80.6 2.5 copy.55
  83.1 1.3 fusion.41
  86.1 9.2 %fusion.8 = f32[64,240]{1,0:T(8,128)S(1)} fusion(bf16[1,240,16384]{2,1,0:T(8,128)(2,1)} %param.10, f32[64,128,128]{2,0,1:T(8,128)} %bitcast.157, f32[64]{0:T(128)S(1)} %get-tuple-element.14, f32[64]{0:T(128)S(1)} %get-tuple-element.16, f32[64]{0:T(128)S(1)} %get-tuple-element.15), kind=kOutput, calls=%fused_computation.21 | convolution fusion | flops 509607936 | bytes 12120832 | tf_op jit(solution)/shard_map/dot_general | solution.py:47
  96.4 109.5 %all-reduce.5.cloned.1.call-done = f32[40256]{0:T(1024)} async-done(((f32[40256]{0:T(1024)}), f32[40256]{0:T(1024)}) %all-reduce.5.cloned.1.call-update) | async-done | bytes 161040 | tf_op jit(solution)/shard_map/psum | solution.py:189
  205.9 69.0 %all-reduce.7.cloned.1.call-done = f32[40256]{0:T(1024)} async-done(((f32[40256]{0:T(1024)}), f32[40256]{0:T(1024)}) %all-reduce.7.cloned.1.call-update) | async-done | bytes 161040 | tf_op jit(solution)/shard_map/psum | solution.py:189
  274.9 1.6 copy.58
  (88 shorter events, 14.7 us)
Async XLA Ops:
  7.2 12.7 %copy-start = (bf16[128,128]{1,0:T(8,128)(2,1)S(1)}, bf16[128,128]{1,0:T(8,128)(2,1)}, u32[]{:S(2)}) copy-start(bf16[128,128]{1,0:T(8,128)(2,1)} %param.18) | copy-start | bytes 98308
  7.2 198.7 %all-reduce.5.cloned.1.call-start = ((), (), s32[]{:S(2)}) async-start(), calls=%async_computation | async-start | bytes 327680 | tf_op jit(solution)/shard_map/psum | solution.py:189
  12.8 7.1 %copy-start.1 = (f32[64,128,128]{2,0,1:T(8,128)}, f32[64,128,128]{2,0,1:T(8,128)S(1)}, u32[]{:S(2)}) copy-start(f32[64,128,128]{2,0,1:T(8,128)S(1)} %fusion.5) | copy-start | bytes 12582916
  19.8 4.6 %copy-start.5 = (bf16[128,16384]{0,1:T(8,128)(2,1)}, bf16[128,16384]{0,1:T(8,128)(2,1)S(1)}, u32[]{:S(2)}) copy-start(bf16[128,16384]{0,1:T(8,128)(2,1)S(1)} %get-tuple-element.37) | copy-start | bytes 12582916
  19.8 6.6 %copy-start.8 = (bf16[128]{0:T(256)(128)(2,1)S(1)}, bf16[128]{0:T(256)(128)(2,1)}, u32[]{:S(2)}) copy-start(bf16[128]{0:T(256)(128)(2,1)} %param.19) | copy-start | bytes 772
  24.5 3.4 %copy-start.7 = (s32[1,384]{1,0:T(1,128)S(1)}, s32[1,384]{1,0:T(1,128)}, u32[]{:S(2)}) copy-start(s32[1,384]{1,0:T(1,128)} %param.13) | copy-start | bytes 4612
  24.5 3.5 %copy-start.10 = (s32[1,8]{1,0:T(1,128)S(1)}, s32[1,8]{1,0:T(1,128)}, u32[]{:S(2)}) copy-start(s32[1,8]{1,0:T(1,128)} %param.12) | copy-start | bytes 100
  24.5 21.7 %copy-start.9 = (s32[1,12]{1,0:T(1,128)S(1)}, s32[1,12]{1,0:T(1,128)}, u32[]{:S(2)}) copy-start(s32[1,12]{1,0:T(1,128)} %param.14) | copy-start | bytes 148
  28.5 7.6 %collective-permute-start.3 = (f32[4]{0:T(128)S(1)}, f32[4]{0:T(128)S(1)}, u32[]{:S(2)}, u32[]{:S(2)}) collective-permute-start(f32[4]{0:T(128)S(1)} %get-tuple-element.26), channel_id=1, source_target_pairs={{0,1},{1,2},{2,3},{3,4},{4,5},{5,6},{6,7},{7,8},{8,9},{9,10},{10,1... | collective-permute-start | bytes 56 | tf_op jit(solution)/shard_map/ppermute | solution.py:12
  31.2 7.0 %collective-permute-start.4 = (f32[4]{0:T(128)S(1)}, f32[4]{0:T(128)S(1)}, u32[]{:S(2)}, u32[]{:S(2)}) collective-permute-start(f32[4]{0:T(128)S(1)} %get-tuple-element.25), channel_id=1, source_target_pairs={{0,2},{1,3},{2,4},{3,5},{4,6},{5,7},{6,8},{7,9},{8,10},{9,11},{10,... | collective-permute-start | bytes 56 | tf_op jit(solution)/shard_map/ppermute | solution.py:12
  32.5 6.3 %collective-permute-start.5 = (f32[4]{0:T(128)S(1)}, f32[4]{0:T(128)S(1)}, u32[]{:S(2)}, u32[]{:S(2)}) collective-permute-start(f32[4]{0:T(128)S(1)} %get-tuple-element.24), channel_id=1, source_target_pairs={{0,3},{1,4},{2,5},{3,6},{4,7},{5,8},{6,9},{7,10},{8,11},{9,12},{10... | collective-permute-start | bytes 56 | tf_op jit(solution)/shard_map/ppermute | solution.py:12
  34.3 5.4 %collective-permute-start = (f32[4]{0:T(128)S(1)}, f32[4]{0:T(128)S(1)}, u32[]{:S(2)}, u32[]{:S(2)}) collective-permute-start(f32[4]{0:T(128)S(1)} %get-tuple-element.30), channel_id=1, source_target_pairs={{0,1},{1,2},{2,3},{3,4},{4,5},{5,6},{6,7},{7,8},{8,9},{9,10},{10,1... | collective-permute-start | bytes 56 | tf_op jit(solution)/shard_map/ppermute | solution.py:12
  34.7 7.1 %collective-permute-start.1 = (f32[4]{0:T(128)S(1)}, f32[4]{0:T(128)S(1)}, u32[]{:S(2)}, u32[]{:S(2)}) collective-permute-start(f32[4]{0:T(128)S(1)} %get-tuple-element.29), channel_id=1, source_target_pairs={{0,2},{1,3},{2,4},{3,5},{4,6},{5,7},{6,8},{7,9},{8,10},{9,11},{10,... | collective-permute-start | bytes 56 | tf_op jit(solution)/shard_map/ppermute | solution.py:12
  36.1 6.3 %collective-permute-start.2 = (f32[4]{0:T(128)S(1)}, f32[4]{0:T(128)S(1)}, u32[]{:S(2)}, u32[]{:S(2)}) collective-permute-start(f32[4]{0:T(128)S(1)} %get-tuple-element.28), channel_id=1, source_target_pairs={{0,3},{1,4},{2,5},{3,6},{4,7},{5,8},{6,9},{7,10},{8,11},{9,12},{10... | collective-permute-start | bytes 56 | tf_op jit(solution)/shard_map/ppermute | solution.py:12
  38.3 4.3 %collective-permute-start.6 = (f32[4]{0:T(128)S(1)}, f32[4]{0:T(128)S(1)}, u32[]{:S(2)}, u32[]{:S(2)}) collective-permute-start(f32[4]{0:T(128)S(1)} %get-tuple-element.34), channel_id=1, source_target_pairs={{0,1},{1,2},{2,3},{3,4},{4,5},{5,6},{6,7},{7,8},{8,9},{9,10},{10,1... | collective-permute-start | bytes 56 | tf_op jit(solution)/shard_map/ppermute | solution.py:12
  38.8 5.7 %collective-permute-start.7 = (f32[4]{0:T(128)S(1)}, f32[4]{0:T(128)S(1)}, u32[]{:S(2)}, u32[]{:S(2)}) collective-permute-start(f32[4]{0:T(128)S(1)} %get-tuple-element.33), channel_id=1, source_target_pairs={{0,2},{1,3},{2,4},{3,5},{4,6},{5,7},{6,8},{7,9},{8,10},{9,11},{10,... | collective-permute-start | bytes 56 | tf_op jit(solution)/shard_map/ppermute | solution.py:12
  39.7 6.3 %collective-permute-start.8 = (f32[4]{0:T(128)S(1)}, f32[4]{0:T(128)S(1)}, u32[]{:S(2)}, u32[]{:S(2)}) collective-permute-start(f32[4]{0:T(128)S(1)} %get-tuple-element.32), channel_id=1, source_target_pairs={{0,3},{1,4},{2,5},{3,6},{4,7},{5,8},{6,9},{7,10},{8,11},{9,12},{10... | collective-permute-start | bytes 56 | tf_op jit(solution)/shard_map/ppermute | solution.py:12
  47.0 3.2 %collective-permute-start.9 = (f32[4]{0:T(128)S(1)}, f32[4]{0:T(128)S(1)}, u32[]{:S(2)}, u32[]{:S(2)}) collective-permute-start(f32[4]{0:T(128)S(1)} %get-tuple-element.22), channel_id=1, source_target_pairs={{0,31},{1,0},{2,1},{3,2},{4,3},{5,4},{6,5},{7,6},{8,7},{9,8},{10,9... | collective-permute-start | bytes 56 | tf_op jit(solution)/shard_map/ppermute | solution.py:12
  47.9 2.7 collective-permute-start.10
  49.9 4.5 %collective-permute-start.11 = (f32[4]{0:T(128)S(1)}, f32[4]{0:T(128)S(1)}, u32[]{:S(2)}, u32[]{:S(2)}) collective-permute-start(f32[4]{0:T(128)S(1)} %get-tuple-element.20), channel_id=1, source_target_pairs={{0,29},{1,30},{2,31},{3,0},{4,1},{5,2},{6,3},{7,4},{8,5},{9,6},{10... | collective-permute-start | bytes 56 | tf_op jit(solution)/shard_map/ppermute | solution.py:12
  54.9 10.0 %copy-start.6 = (bf16[128,16384]{0,1:T(8,128)(2,1)S(1)}, bf16[128,16384]{0,1:T(8,128)(2,1)}, u32[]{:S(2)}) copy-start(bf16[128,16384]{0,1:T(8,128)(2,1)} %copy-done.5) | copy-start | bytes 12582916
  54.9 11.4 %slice-start = ((s8[8388608]{0:T(1024)(128)(4,1)}), s8[4194304]{0:T(1024)(128)(4,1)S(1)}, s32[]{:S(2)}) async-start(s8[8388608]{0:T(1024)(128)(4,1)} %bitcast.177), calls=%async_computation.2 | async-start | bytes 8388608
  67.1 7.6 %copy-start.2 = (f32[64,128,128]{2,0,1:T(8,128)S(1)}, f32[64,128,128]{2,0,1:T(8,128)}, u32[]{:S(2)}) copy-start(f32[64,128,128]{2,0,1:T(8,128)} %copy-done.1) | copy-start | bytes 12582916
  96.3 178.6 %all-reduce.7.cloned.1.call-start = ((), (), s32[]{:S(2)}) async-start(), calls=%async_computation.1 | async-start | bytes 327680 | tf_op jit(solution)/shard_map/psum | solution.py:189
  (5 other events, 12.1 us)
Sparse Core Ops, SparseCore 0:
  96.5 109.3 all-reduce.4
  208.2 66.6 all-reduce.6
